TPU v7x, 256 devices: a whole 4x4x8 slice. The times are simulated.
256 devices in a mesh: inst: 16 (over x, y), page: 8 (over z), head: 2 (over core).
Axes of the slice: x: 4, y: 4, z: 8, core: 2. Of those that a mesh axis runs over, the one named last changes fastest.
Arguments:
- queries: bfloat16 [32, 8192], P('inst', 'head'), may hold values from -21 to 21
- fresh_key_value: bfloat16 [2, 32, 1024], P(None, 'inst', 'head'), may hold values from -8 to 8
- key_value_pool: bfloat16 [2, 16384, 16, 1024], P(None, ('inst', 'page'), None, 'head'), may hold values from -21 to 21
- block_table: int32 [32, 768], P('inst'), may hold values from -1 to 16383, as said below
- lengths: int32 [32], P('inst'), may hold values from 17 to 12288, as said below
Outputs:
- attn: bfloat16 [32, 8192], P('inst', 'head')
Inputs may be any that keep to these rules, and one draw needn't show every extreme that they name: `block_table`: request r is owned by instance r // 2. Entries 0 to ceil(lengths[r] / 16) - 1 of row r are pool page numbers below 16384, distinct over all requests; every other entry is -1. `lengths`: every request has two or more pages; some request has exactly 768 full pages.
All inputs are finite; a program needn't handle non-finite values.
Results may differ from a plain program's by a relative error of at most 0.001.
Values may be sent and summed in bfloat16 or wider, within the bound.
No kernel may reach another device: no remote copies, remote signals or barrier semaphores. Data moves between devices by JAX's collectives and lax.ppermute only.
A program may use at most 192 MiB of HBM per device.

v0:
```python
import math
import jax
import jax.numpy as jnp
from jax import lax
from jax.sharding import PartitionSpec as P

HEAD_SIZE = 128
LOWEST_SCORE = -1e30


def slot_owners(all_tables, all_lengths, slots, page_tok):
    requests, most_pages = all_tables.shape
    first_page = (lax.axis_index("inst") * lax.axis_size("page") + lax.axis_index("page")) * slots
    column = jnp.arange(most_pages, dtype=jnp.int32)
    live_page = column[None, :] * page_tok < all_lengths[:, None]
    local_page = all_tables - first_page
    inside = live_page & (local_page >= 0) & (local_page < slots)
    expected_output = jnp.where(inside, local_page, slots).reshape(-1)
    request_ids = jnp.broadcast_to(
        jnp.arange(requests, dtype=jnp.int32)[:, None], (requests, most_pages)
    ).reshape(-1)
    page_fill = jnp.clip(all_lengths[:, None] - column[None, :] * page_tok, 0, page_tok).reshape(-1)
    page_owner = (
        jnp.full((slots,), requests, jnp.int32).at[expected_output].set(request_ids, mode="drop")
    )
    filled = jnp.zeros((slots,), jnp.int32).at[expected_output].set(page_fill, mode="drop")
    return (page_owner, filled)


def page_partials(slot_queries, key_value_pool, filled):
    slots = key_value_pool.shape[1]
    page_tok = key_value_pool.shape[2]
    groups = key_value_pool.shape[3] // HEAD_SIZE
    heads = slot_queries.shape[1] // HEAD_SIZE
    grouped_queries = slot_queries.reshape(slots, groups, heads // groups, HEAD_SIZE)
    paged_keys = key_value_pool[0].reshape(slots, page_tok, groups, HEAD_SIZE)
    paged_values = key_value_pool[1].reshape(slots, page_tok, groups, HEAD_SIZE)
    scores = jnp.einsum(
        "sgqd,stgd->sgqt", grouped_queries, paged_keys, preferred_element_type=jnp.float32
    ) * (1.0 / math.sqrt(HEAD_SIZE))
    offsets = jnp.arange(page_tok, dtype=jnp.int32)
    valid = (offsets[None, :] < filled[:, None])[:, None, None, :]
    masked = jnp.where(valid, scores, LOWEST_SCORE)
    page_max = jnp.max(masked, axis=3)
    raw_weight = jnp.where(valid, jnp.exp(masked - page_max[..., None]), 0.0)
    page_sum = jnp.sum(raw_weight, axis=3)
    page_out = jnp.einsum(
        "sgqt,stgd->sgqd",
        raw_weight.astype(jnp.bfloat16),
        paged_values,
        preferred_element_type=jnp.float32,
    )
    return (
        page_max.reshape(slots, heads),
        page_sum.reshape(slots, heads),
        page_out.reshape(slots, heads * HEAD_SIZE),
    )


def request_max(page_max, page_owner, requests):
    matches = page_owner[None, :] == jnp.arange(requests, dtype=jnp.int32)[:, None]
    return jnp.max(jnp.where(matches[:, :, None], page_max[None], LOWEST_SCORE), axis=1)


def request_sums(page_max, page_sum, page_out, page_owner, shared_max):
    requests, heads = shared_max.shape
    slots = page_max.shape[0]
    padded = jnp.concatenate([shared_max, jnp.full((1, heads), LOWEST_SCORE, jnp.float32)], axis=0)
    factor = jnp.exp(page_max - padded[page_owner])
    one_hot = (page_owner[None, :] == jnp.arange(requests, dtype=jnp.int32)[:, None]).astype(
        jnp.float32
    )
    scaled_out = (page_out.reshape(slots, heads, HEAD_SIZE) * factor[:, :, None]).reshape(
        slots, heads * HEAD_SIZE
    )
    summed_out = jnp.dot(
        one_hot, scaled_out, precision=lax.Precision.HIGHEST, preferred_element_type=jnp.float32
    )
    summed_total = jnp.dot(
        one_hot,
        page_sum * factor,
        precision=lax.Precision.HIGHEST,
        preferred_element_type=jnp.float32,
    )
    return (summed_total, summed_out)


def finish(queries, fresh_key_value, cache_max, cache_total, cache_out):
    own_rows = queries.shape[0]
    heads = queries.shape[1] // HEAD_SIZE
    groups = fresh_key_value.shape[2] // HEAD_SIZE
    per_group = heads // groups
    grouped_queries = queries.reshape(own_rows, groups, per_group, HEAD_SIZE)
    new_keys = fresh_key_value[0].reshape(own_rows, groups, HEAD_SIZE)
    fresh_score = jnp.einsum(
        "rgqd,rgd->rgq", grouped_queries, new_keys, preferred_element_type=jnp.float32
    ).reshape(own_rows, heads) * (1.0 / math.sqrt(HEAD_SIZE))
    top_score = jnp.maximum(cache_max, fresh_score)
    carried = jnp.exp(cache_max - top_score)
    own_weight = jnp.exp(fresh_score - top_score)
    denominator = own_weight + cache_total * carried
    new_values = jnp.broadcast_to(
        fresh_key_value[1].astype(jnp.float32).reshape(own_rows, groups, 1, HEAD_SIZE),
        (own_rows, groups, per_group, HEAD_SIZE),
    ).reshape(own_rows, heads, HEAD_SIZE)
    weighted = (
        own_weight[:, :, None] * new_values
        + cache_out.reshape(own_rows, heads, HEAD_SIZE) * carried[:, :, None]
    )
    return (
        (weighted / denominator[:, :, None])
        .reshape(own_rows, heads * HEAD_SIZE)
        .astype(jnp.bfloat16)
    )


def shards(queries, fresh_key_value, key_value_pool, block_table, lengths):
    all_tables, all_lengths = (
        lax.all_gather(block_table, "inst", axis=0, tiled=True),
        lax.all_gather(lengths, "inst", axis=0, tiled=True),
    )
    all_queries = lax.all_gather(queries, "inst", axis=0, tiled=True)
    requests = all_tables.shape[0]
    own_rows = queries.shape[0]
    row_start = lax.axis_index("inst") * own_rows
    page_owner, filled = slot_owners(
        all_tables, all_lengths, key_value_pool.shape[1], key_value_pool.shape[2]
    )
    slot_queries = all_queries[jnp.minimum(page_owner, requests - 1)]
    page_max, page_sum, page_out = page_partials(slot_queries, key_value_pool, filled)
    local_max = request_max(page_max, page_owner, requests)
    shared_max = lax.pmax(local_max, ("inst", "page"))
    shared_total, shared_out = request_sums(page_max, page_sum, page_out, page_owner, shared_max)
    summed_out, summed_total = lax.psum((shared_out, shared_total), ("inst", "page"))
    cache_max = lax.dynamic_slice_in_dim(shared_max, row_start, own_rows, 0)
    cache_total = lax.dynamic_slice_in_dim(summed_total, row_start, own_rows, 0)
    cache_out = lax.dynamic_slice_in_dim(summed_out, row_start, own_rows, 0)
    return finish(queries, fresh_key_value, cache_max, cache_total, cache_out)


def solution(mesh):
    return jax.shard_map(
        shards,
        mesh=mesh,
        in_specs=(
            P("inst", "head"),
            P(None, "inst", "head"),
            P(None, ("inst", "page"), None, "head"),
            P("inst", None),
            P("inst"),
        ),
        out_specs=P("inst", "head"),
        check_vma=False,
    )
```

profile of v0, /device:TPU:0, one launch (start us, length us, event | category | flops | bytes accessed | tf_op | source)
XLA Modules:
  0.0 1664.2 jit_solution(2714726597789726109)
XLA Ops:
  6.5 1.3 dynamic-slice
  8.5 0.9 dynamic-update-slice
  9.3 14.7 all-reduce.1
  24.0 21.6 %all-gather = s32[16,2,768]{2,1,0:T(2,128)S(1)} all-gather(s32[1,2,768]{2,1,0:T(2,128)} %bitcast.89), channel_id=1, replica_groups=mesh['inst'=16,'page'=8,'head'=2] {'inst'}, dimensions={0}, use_global_device_ids=true | all-gather | bytes 104448 | tf_op jit(solution)/shard_map/all_gather | solution.py:119
  45.8 0.1 subtract_clamp_fusion
  45.9 0.1 copy.36
  46.0 0.1 compare_select_fusion
  46.1 90.2 %scatter_custom_fusion = s32[128]{0:T(128)S(1)} fusion(s32[24576]{0:T(1024)S(1)} %bitcast.84, s32[24576]{0:T(1024)S(1)} %reshape.155, s32[]{:T(128)} %constant.17.clone.1), kind=kCustom, calls=%fused_computation.59 | custom fusion | bytes 516 | tf_op jit(solution)/shard_map/scatter | solution.py:24
  136.3 90.2 %scatter_custom_fusion.1 = s32[128]{0:T(128)S(1)} fusion(s32[24576]{0:T(1024)S(1)} %bitcast.85, s32[24576]{0:T(1024)S(1)} %reshape.163, s32[]{:T(128)} %constant.5.clone.1), kind=kCustom, calls=%fused_computation.57 | custom fusion | bytes 516 | tf_op jit(solution)/shard_map/scatter | solution.py:26
  226.6 22.9 %all-gather.1 = bf16[16,2,4096]{2,1,0:T(2,128)(2,1)S(1)} all-gather(bf16[1,2,4096]{2,1,0:T(2,128)(2,1)} %bitcast.87), channel_id=1, replica_groups=mesh['inst'=16,'page'=8,'head'=2] {'inst'}, dimensions={0}, use_global_device_ids=true | all-gather | bytes 278528 | tf_op jit(solution)/shard_map/all_gather | solution.py:122
  249.6 1.2 gather_fusion
  250.8 0.2 copy.37
  251.0 4.6 fusion.34
  255.6 3.5 copy.34
  259.1 3.0 copy.27
  262.1 3.5 copy.33
  265.6 3.0 copy.24
  268.5 2.9 fusion.4
  271.6 0.1 copy.28
  271.7 0.2 select_reduce_fusion
  271.9 689.7 %pmax.7 = f32[32,32]{1,0:T(8,128)S(1)} all-reduce(f32[32,32]{1,0:T(8,128)S(1)} %select_reduce_fusion), channel_id=1, replica_groups=mesh['inst'=16,'page'=8,'head'=2] {'inst','page'}, use_global_device_ids=true, to_apply=%region_4.5 | all-reduce | flops 1024 | bytes 8192 | tf_op jit(solution)/shard_map/pmax | solution.py:132
  961.6 3.7 fusion.7
  965.3 0.6 gather_fusion.1
  966.0 0.6 mul.86
  966.6 1.0 copy-done
  967.6 4.3 fusion
  971.9 1.4 fusion.5
  973.3 0.1 fusion.18
  973.6 0.1 copy.30
  973.8 0.1 fusion.14
  973.9 681.6 %psum.15 = f32[32,32]{1,0:T(8,128)S(1)} all-reduce(f32[32,32]{1,0:T(8,128)S(1)} %fusion.14), channel_id=1, replica_groups=mesh['inst'=16,'page'=8,'head'=2] {'inst','page'}, use_global_device_ids=true, to_apply=%region_7.8 | all-reduce | flops 1024 | bytes 8192 | tf_op jit(solution)/shard_map/psum | solution.py:134
  1655.7 1.6 fusion.17
  (34 shorter events, 0.8 us)
Async XLA Ops:
  6.5 1649.2 %all-reduce.4.cloned.1.call-start = ((), (), s32[]{:S(2)}) async-start(), calls=%async_computation | async-start | bytes 1048576 | tf_op jit(solution)/shard_map/psum | solution.py:134
  966.0 1.6 copy-start
  971.9 1.4 copy-start.2
  971.9 1.4 copy-start.1
Sparse Core Ops, SparseCore 0:
  972.0 207.2 all-reduce.3
where the time goes:
time: 1660 us
  blocking collectives  1430 us (86%)
  local copies, waits for them, and re-layouts  205 us (12%)
    pmax x1, blocking collectives, shards(): shared_max = lax.pmax(local_max, ('inst', 'page'))  690 us
    psum x1, blocking collectives, shards(): lax.psum((shared_out, shared_total), ('inst', 'page'))  682 us
    scatter x1, local copies, waits for them, and re-layouts, slot_owners(): jnp.full((slots,), requests, jnp.int32).at[expected_output]  90.2 us
    scatter x1, local copies, waits for them, and re-layouts, slot_owners(): jnp.zeros((slots,), jnp.int32).at[expected_output]  90.2 us
  transfers between devices with their start and end apart: 1, of which 0 were waited for; matrix products, arithmetic and copies ran while one was open for 0% of the time, Pallas kernels for 0%

commit v1 on v0

--- a/solution.py
+++ b/solution.py
@@ -131,7 +131,7 @@
     local_max = request_max(page_max, page_owner, requests)
     shared_max = lax.pmax(local_max, ("inst", "page"))
     shared_total, shared_out = request_sums(page_max, page_sum, page_out, page_owner, shared_max)
-    summed_out, summed_total = lax.psum((shared_out, shared_total), ("inst", "page"))
+    summed_out, summed_total = lax.psum(lax.psum((shared_out, shared_total), "page"), "inst")
     cache_max = lax.dynamic_slice_in_dim(shared_max, row_start, own_rows, 0)
     cache_total = lax.dynamic_slice_in_dim(summed_total, row_start, own_rows, 0)
     cache_out = lax.dynamic_slice_in_dim(summed_out, row_start, own_rows, 0)

time: 1660 us -> 1170 us (0.70)
  blocking collectives: 1430 us -> 845 us
  waiting for transfers between devices: 0.04 us -> 87.6 us
    psum x1 -> x2, blocking collectives: 682 us -> 96.6 us  [the longest x1 69.5 us: shards(): lax.psum(lax.psum((shared_out, shared_total), 'page'), 'inst')]
    psum x1 -> x2, waiting for transfers between devices: 0.02 us -> 87.6 us  [the longest x1 87.6 us: shards(): lax.psum(lax.psum((shared_out, shared_total), 'page'), 'inst')]
  transfers between devices with their start and end apart: 1 -> 2, of which waited for: 0 -> 1; matrix products, arithmetic and copies ran while one was open for 0% -> 0% of each run, Pallas kernels for 0% -> 0%
where the time goes in v1:
time: 1170 us
  blocking collectives  845 us (72%)
  local copies, waits for them, and re-layouts  205 us (18%)
  waiting for transfers between devices  87.6 us (7%)
  between operations  14.3 us (1%)
    pmax x1, blocking collectives, shards(): shared_max = lax.pmax(local_max, ('inst', 'page'))  690 us
    scatter x1, local copies, waits for them, and re-layouts, slot_owners(): jnp.full((slots,), requests, jnp.int32).at[expected_output]  90.2 us
    scatter x1, local copies, waits for them, and re-layouts, slot_owners(): jnp.zeros((slots,), jnp.int32).at[expected_output]  90.2 us
    psum x1, waiting for transfers between devices, shards(): lax.psum(lax.psum((shared_out, shared_total), 'page'), 'inst')  87.6 us
    psum x1, blocking collectives, shards(): lax.psum(lax.psum((shared_out, shared_total), 'page'), 'inst')  69.5 us
    psum x1, blocking collectives, shards(): lax.psum((shared_out, shared_total), 'page')  27.1 us
  transfers between devices with their start and end apart: 2, of which 1 were waited for; matrix products, arithmetic and copies ran while one was open for 0% of the time, Pallas kernels for 0%

profile of v1, /device:TPU:0, one launch (start us, length us, event | category | flops | bytes accessed | tf_op | source)
XLA Modules:
  0.0 1166.8 jit_solution(13261194738452508063)
XLA Ops:
  6.5 1.3 dynamic-slice
  8.5 0.9 dynamic-update-slice
  9.3 14.7 %all-reduce.1 = s32[32]{0:T(128)S(1)} all-reduce(s32[32]{0:T(128)S(1)} %dynamic-update-slice), channel_id=1, replica_groups=mesh['inst'=16,'page'=8,'head'=2] {'inst'}, use_global_device_ids=true, to_apply=%add.1 | all-reduce | flops 32 | bytes 256
  24.0 21.6 %all-gather = s32[16,2,768]{2,1,0:T(2,128)S(1)} all-gather(s32[1,2,768]{2,1,0:T(2,128)} %bitcast.89), channel_id=1, replica_groups=mesh['inst'=16,'page'=8,'head'=2] {'inst'}, dimensions={0}, use_global_device_ids=true | all-gather | bytes 104448 | tf_op jit(solution)/shard_map/all_gather | solution.py:119
  46.0 0.1 compare_select_fusion
  46.1 90.2 %scatter_custom_fusion = s32[128]{0:T(128)S(1)} fusion(s32[24576]{0:T(1024)S(1)} %bitcast.84, s32[24576]{0:T(1024)S(1)} %reshape.155, s32[]{:T(128)} %constant.17.clone.1), kind=kCustom, calls=%fused_computation.59 | custom fusion | bytes 516 | tf_op jit(solution)/shard_map/scatter | solution.py:24
  136.3 90.2 %scatter_custom_fusion.1 = s32[128]{0:T(128)S(1)} fusion(s32[24576]{0:T(1024)S(1)} %bitcast.85, s32[24576]{0:T(1024)S(1)} %reshape.163, s32[]{:T(128)} %constant.5.clone.1), kind=kCustom, calls=%fused_computation.57 | custom fusion | bytes 516 | tf_op jit(solution)/shard_map/scatter | solution.py:26
  226.6 22.9 %all-gather.1 = bf16[16,2,4096]{2,1,0:T(2,128)(2,1)S(1)} all-gather(bf16[1,2,4096]{2,1,0:T(2,128)(2,1)} %bitcast.87), channel_id=1, replica_groups=mesh['inst'=16,'page'=8,'head'=2] {'inst'}, dimensions={0}, use_global_device_ids=true | all-gather | bytes 278528 | tf_op jit(solution)/shard_map/all_gather | solution.py:122
  249.6 1.2 gather_fusion
  250.8 0.2 copy.37
  251.0 4.6 fusion.34
  255.6 3.5 copy.34
  259.1 3.0 copy.27
  262.1 3.5 copy.33
  265.6 3.0 copy.24
  268.5 2.9 fusion.4
  271.6 0.1 copy.28
  271.7 0.2 select_reduce_fusion
  271.9 689.7 %pmax.7 = f32[32,32]{1,0:T(8,128)S(1)} all-reduce(f32[32,32]{1,0:T(8,128)S(1)} %select_reduce_fusion), channel_id=1, replica_groups=mesh['inst'=16,'page'=8,'head'=2] {'inst','page'}, use_global_device_ids=true, to_apply=%region_4.5 | all-reduce | flops 1024 | bytes 8192 | tf_op jit(solution)/shard_map/pmax | solution.py:132
  961.6 3.7 fusion.7
  965.3 0.6 gather_fusion.1
  966.0 0.6 mul.86
  966.6 1.0 copy-done
  967.5 4.3 fusion
  971.9 1.4 fusion.5
  973.4 0.1 fusion.18
  973.7 0.1 copy.30
  973.8 0.1 fusion.14
  974.0 27.1 %psum.30 = f32[32,32]{1,0:T(8,128)S(1)} all-reduce(f32[32,32]{1,0:T(8,128)S(1)} %fusion.14), channel_id=1, replica_groups=mesh['inst'=16,'page'=8,'head'=2] {'page'}, use_global_device_ids=true, to_apply=%region_8.9 | all-reduce | flops 1024 | bytes 8192 | tf_op jit(solution)/shard_map/psum | solution.py:134
  1001.0 69.5 %psum.31 = f32[32,32]{1,0:T(8,128)S(1)} all-reduce(f32[32,32]{1,0:T(8,128)S(1)} %psum.30), channel_id=1, replica_groups=mesh['inst'=16,'page'=8,'head'=2] {'inst'}, use_global_device_ids=true, to_apply=%region_9.10 | all-reduce | flops 1024 | bytes 8192 | tf_op jit(solution)/shard_map/psum | solution.py:134
  1070.8 87.6 %all-reduce.7.cloned.1.call-done = f32[32,4096]{1,0:T(8,128)} async-done(((f32[32,4096]{1,0:T(8,128)}), f32[32,4096]{1,0:T(8,128)}) %all-reduce.7.cloned.1.call-update) | async-done | bytes 524304 | tf_op jit(solution)/shard_map/psum | solution.py:134
  1158.4 1.6 fusion.17
  (38 shorter events, 1.1 us)
Async XLA Ops:
  6.5 1064.0 %all-reduce.5.cloned.1.call-start = ((), (), s32[]{:S(2)}) async-start(), calls=%async_computation | async-start | bytes 1048576 | tf_op jit(solution)/shard_map/psum | solution.py:134
  966.0 1.6 copy-start
  971.9 1.5 copy-start.2
  971.9 1.5 copy-start.1
  971.9 186.5 %all-reduce.7.cloned.1.call-start = ((), (), s32[]{:S(2)}) async-start(), calls=%async_computation.1 | async-start | bytes 1048576 | tf_op jit(solution)/shard_map/psum | solution.py:134
Sparse Core Ops, SparseCore 0:
  972.0 64.1 all-reduce.4
  1070.7 87.5 all-reduce.6
